TPU v7x, 512 devices: a whole 4x8x8 slice. The times are simulated.
512 devices in a mesh: req: 128 (over y, z, core), tp: 4 (over x).
Axes of the slice: x: 4, y: 8, z: 8, core: 2. Of those that a mesh axis runs over, the one named last changes fastest.
Arguments:
- attn_out: bfloat16 [8192, 2048], P('req', 'tp'), may hold values from -6 to 6
- w_out: bfloat16 [2048, 2048], P('tp'), may hold values from -0.125 to 0.125
- residual: bfloat16 [8192, 2048], P('req', 'tp'), may hold values from -6 to 6
- routes: int32 [8192, 6], P('req'), may hold values from 0 to 127, all different within a row; in each aligned block of 64 rows (0 to 63, 64 to 127, ...) at most 6 rows name the same one
- gates: float32 [8192, 6], P('req'), may hold values from 0.05 to 1
- w_gate: bfloat16 [128, 2048, 1024], P('req', None, 'tp'), as said below
- w_up: bfloat16 [128, 2048, 1024], P('req', None, 'tp'), as said below
- w_down: bfloat16 [128, 1024, 2048], P('req', None, 'tp'), as said below
- norm_gain: float32 [2048], P('tp'), may hold values from 0.1 to 1.9
Outputs:
- normed: bfloat16 [8192, 2048], P('req', 'tp')
Inputs may be any that keep to these rules, and one draw needn't show every extreme that they name: `routes`: each row names 6 different slots. In the 64 rows of one index of req no slot is named by more than 6 rows, a bound that some block reaches. `w_gate`: slots 2 e and 2 e + 1 hold the same expert e: their weights are equal. `w_up`: slots 2 e and 2 e + 1 hold the same expert e: their weights are equal. `w_down`: slots 2 e and 2 e + 1 hold the same expert e: their weights are equal.
All inputs are finite; a program needn't handle non-finite values.
Results may differ from a plain program's by a relative error of at most 0.0056.
Values may be sent and summed in bfloat16 or wider, within the bound.
A program may use at most 64 MiB of HBM per device.

v0:
```python
import jax
import jax.numpy as jnp
from jax import lax
from jax.sharding import PartitionSpec as P


def body(attn_out, w_out, residual, routes, gates, w_gate, w_up, w_down, norm_gain):
    row_count = attn_out.shape[0]
    part_width = residual.shape[1]
    full_width = w_out.shape[1]
    route_count = routes.shape[1]
    slot_count = lax.axis_size("req")
    capacity = max(2, min(row_count, 2 * row_count * route_count // slot_count))
    tp_index = lax.axis_index("tp")
    partial_value = jnp.dot(attn_out, w_out, preferred_element_type=jnp.float32)
    own_block = lax.dynamic_slice_in_dim(partial_value, tp_index * part_width, part_width, 1)
    partial_value = lax.dynamic_update_slice_in_dim(
        partial_value, own_block + residual.astype(jnp.float32), tp_index * part_width, 1
    )
    flat_routes = routes.reshape(-1)
    one_hot = (flat_routes[:, None] == jnp.arange(slot_count, dtype=jnp.int32)[None, :]).astype(
        jnp.int32
    )
    position = jnp.sum(one_hot * (jnp.cumsum(one_hot, axis=0) - 1), axis=1)
    dest_index = flat_routes * capacity + position
    row_ids = jnp.repeat(jnp.arange(row_count, dtype=jnp.int32), route_count)
    source_row = jnp.zeros((slot_count * capacity,), jnp.int32).at[dest_index].set(row_ids)
    gate_local = w_gate[0]
    up_local = w_up[0]
    down_local = w_down[0]
    projected = lax.psum(partial_value, "tp")
    own_part = lax.dynamic_slice_in_dim(projected, tp_index * part_width, part_width, 1)
    outgoing = projected.astype(jnp.bfloat16)[source_row].reshape(slot_count, capacity, full_width)
    incoming = lax.all_to_all(outgoing, "req", split_axis=0, concat_axis=0, tiled=True)
    expert_rows = incoming.reshape(slot_count * capacity, full_width)
    gate_act = jnp.dot(expert_rows, gate_local, preferred_element_type=jnp.float32)
    up_act = jnp.dot(expert_rows, up_local, preferred_element_type=jnp.float32)
    hidden = (jax.nn.silu(gate_act) * up_act).astype(jnp.bfloat16)
    expert_out = jnp.dot(
        lax.all_gather(hidden, "tp", axis=1, tiled=True),
        down_local,
        preferred_element_type=jnp.float32,
    )
    expert_out = expert_out.astype(jnp.bfloat16).reshape(slot_count, capacity, down_local.shape[1])
    returned = lax.all_to_all(expert_out, "req", split_axis=0, concat_axis=0, tiled=True)
    picked = returned.reshape(slot_count * capacity, part_width)[dest_index]
    picked = picked.reshape(row_count, route_count, part_width).astype(jnp.float32)
    routed_sum = jnp.sum(picked * gates[:, :, None], axis=1)
    combined = own_part + routed_sum
    square_part = jnp.sum(combined * combined, axis=1)
    square_total = lax.psum(square_part, "tp")
    scale = lax.rsqrt(square_total / full_width + 1e-06)
    return (combined * scale[:, None] * norm_gain[None, :]).astype(jnp.bfloat16)


def solution(mesh):
    placed = (
        P("req", "tp"),
        P("tp", None),
        P("req", "tp"),
        P("req", None),
        P("req", None),
        P("req", None, "tp"),
        P("req", None, "tp"),
        P("req", None, "tp"),
        P("tp"),
    )
    return jax.shard_map(
        body, mesh=mesh, in_specs=placed, out_specs=P("req", "tp"), check_vma=False
    )
```

profile of v0, /device:TPU:8, one launch (start us, length us, event | category | flops | bytes accessed | tf_op | source)
XLA Modules:
  0.0 315.9 jit_solution(1539475655118343820)
XLA Ops:
  6.5 0.0 copy-start
  6.5 0.0 all-reduce.2.cloned.1.call-start
  6.5 1.6 copy-done
  8.1 1.3 fusion.12
  9.4 0.9 add_dynamic-update-slice_fusion
  10.3 0.0 copy-start.2
  10.3 0.8 copy-done.2
  11.1 0.0 all-reduce.2.cloned.1.call-update
  11.1 0.0 all-gather.2.cloned.1.call-start
  11.2 0.0 copy-done.3
  11.2 0.1 copy.12
  11.3 0.1 eq.29
  11.4 0.1 eq.25
  11.6 0.1 copy.14
  11.7 0.2 fusion.5
  12.0 0.1 add_add_fusion
  12.0 0.1 copy.11
  12.1 0.1 mul.61
  12.3 0.1 reshape.96
  12.4 0.2 fusion.7
  12.7 2.9 scatter_custom_fusion
  15.6 53.9 %all-reduce.2.cloned.1.call-done = f32[64,2048]{1,0:T(8,128)} async-done(((f32[64,2048]{1,0:T(8,128)}), f32[64,2048]{1,0:T(8,128)}) %all-reduce.2.cloned.1.call-update) | async-done | bytes 524304 | tf_op jit(solution)/shard_map/psum | solution.py:31
  69.5 1.1 convert_element_type.27
  70.6 4.3 %gather_fusion = bf16[768,2048]{1,0:T(8,128)(2,1)} fusion(bf16[64,2048]{1,0:T(8,128)(2,1)S(1)} %convert_element_type.27, s32[1024]{0:T(1024)S(1)} %pad_clamp_fusion.1), kind=kCustom, calls=%fused_computation | custom fusion | bytes 6294528 | tf_op jit(solution)/shard_map/gather | solution.py:33
  74.9 6.3 %reshape.71 = bf16[128,6,2048]{2,1,0:T(8,128)(2,1)} reshape(bf16[768,2048]{1,0:T(8,128)(2,1)} %gather_fusion) | data formatting | bytes 6291456 | tf_op jit(solution)/shard_map/reshape | solution.py:33
  81.1 111.0 %all_to_all.10 = bf16[128,6,2048]{2,1,0:T(8,128)(2,1)} all-to-all(bf16[128,6,2048]{2,1,0:T(8,128)(2,1)} %reshape.71), channel_id=1, replica_groups=mesh['req'=128,'tp'=4] {'req'}, dimensions={0} | all-to-all | bytes 6291456 | tf_op jit(solution)/shard_map/all_to_all | solution.py:34
  192.1 6.3 %reshape.72 = bf16[768,2048]{1,0:T(8,128)(2,1)} reshape(bf16[128,6,2048]{2,1,0:T(8,128)(2,1)} %all_to_all.10) | data formatting | bytes 6291456 | tf_op jit(solution)/shard_map/reshape | solution.py:35
  198.4 3.3 %fusion.3 = f32[768,256]{1,0:T(8,128)S(1)} fusion(bf16[768,2048]{1,0:T(8,128)(2,1)} %reshape.72, bf16[1,2048,256]{2,1,0:T(8,128)(2,1)} %param.14), kind=kOutput, calls=%fused_computation.8 | convolution fusion | flops 805306368 | bytes 4980736 | tf_op jit(solution)/shard_map/dot_general | solution.py:36
  201.7 0.0 copy-done.1
  201.8 0.1 copy-done.6
  201.9 1.7 fusion
  203.6 0.0 all-gather.2.cloned.1.call-update
  203.6 38.7 %all-gather.2.cloned.1.call-done = bf16[768,1024]{1,0:T(8,128)(2,1)} async-done(((bf16[768,256]{1,0:T(8,128)(2,1)}), bf16[768,1024]{1,0:T(8,128)(2,1)}) %all-gather.2.cloned.1.call-update) | async-done | bytes 1572880 | tf_op jit(solution)/shard_map/all_gather | solution.py:40
  242.3 2.7 convolution_convert_fusion
  245.0 0.0 copy-start.4
  245.0 1.3 reshape.73
  246.3 14.6 %all-to-all-start.1 = ((bf16[128,6,512]{2,1,0:T(8,128)(2,1)}), bf16[128,6,512]{2,1,0:T(8,128)(2,1)}, u32[]{:S(2)}, u32[]{:S(2)}) async-start(bf16[128,6,512]{2,1,0:T(8,128)(2,1)} %reshape.73), calls=%async_computation.1 | async-start | bytes 2097152 | tf_op jit(solution)/shard_map/all_to_all | solution.py:45
  260.9 0.0 copy-done.4
  260.9 0.7 copy.16
  261.6 30.2 %all-to-all-done.1 = bf16[128,6,512]{2,1,0:T(8,128)(2,1)} async-done(((bf16[128,6,512]{2,1,0:T(8,128)(2,1)}), bf16[128,6,512]{2,1,0:T(8,128)(2,1)}, u32[]{:S(2)}, u32[]{:S(2)}) %all-to-all-start.1) | async-done | bytes 786464 | tf_op jit(solution)/shard_map/all_to_all | solution.py:45
  291.9 1.4 reshape.74
  293.2 0.0 copy-start.5
  293.3 2.1 gather_fusion.1
  295.3 0.1 reshape.75
  295.4 1.1 multiply_reduce_fusion
  296.6 1.0 multiply_reduce_fusion.1
  297.6 9.8 %psum.15 = f32[64]{0:T(128)S(1)} all-reduce(f32[64]{0:T(128)S(1)} %multiply_reduce_fusion.1), channel_id=1, replica_groups=mesh['req'=128,'tp'=4] {'tp'}, use_global_device_ids=true, to_apply=%region_7.8 | all-reduce | flops 64 | bytes 512 | tf_op jit(solution)/shard_map/psum | solution.py:51
  307.4 1.6 multiply_convert_fusion
  (14 shorter events, 0.1 us)
Async XLA Ops:
  6.5 1.6 copy-start
  6.5 4.6 %copy-start.3 = (s32[64,6]{0,1:T(8,128)S(1)}, s32[64,6]{0,1:T(8,128)}, u32[]{:S(2)}) copy-start(s32[64,6]{0,1:T(8,128)} %param.12) | copy-start | bytes 4612
  6.5 63.0 %all-reduce.2.cloned.1.call-start = ((), (), s32[]{:S(2)}) async-start(), calls=%async_computation.2 | async-start | bytes 1048576 | tf_op jit(solution)/shard_map/psum | solution.py:31
  10.3 0.8 copy-start.2
  11.1 231.1 %all-gather.2.cloned.1.call-start = ((), (), s32[]{:S(2)}) async-start(), calls=%async_computation.3 | async-start | bytes 1966080 | tf_op jit(solution)/shard_map/all_gather | solution.py:40
  198.4 3.3 %copy-start.1 = (bf16[768,2048]{1,0:T(8,128)(2,1)S(1)}, bf16[768,2048]{1,0:T(8,128)(2,1)}, u32[]{:S(2)}) copy-start(bf16[768,2048]{1,0:T(8,128)(2,1)} %reshape.72) | copy-start | bytes 9437188
  198.4 3.4 %copy-start.6 = (bf16[1,2048,256]{2,1,0:T(8,128)(2,1)S(1)}, bf16[1,2048,256]{2,1,0:T(8,128)(2,1)}, u32[]{:S(2)}) copy-start(bf16[1,2048,256]{2,1,0:T(8,128)(2,1)} %param.15) | copy-start | bytes 3145732
  245.0 15.9 %copy-start.4 = (f32[64,6]{0,1:T(8,128)S(1)}, f32[64,6]{0,1:T(8,128)}, u32[]{:S(2)}) copy-start(f32[64,6]{0,1:T(8,128)} %param.13) | copy-start | bytes 4612
  246.3 45.6 %all-to-all-start.1 = ((bf16[128,6,512]{2,1,0:T(8,128)(2,1)}), bf16[128,6,512]{2,1,0:T(8,128)(2,1)}, u32[]{:S(2)}, u32[]{:S(2)}) async-start(bf16[128,6,512]{2,1,0:T(8,128)(2,1)} %reshape.73), calls=%async_computation.1 | async-start | bytes 2097152 | tf_op jit(solution)/shard_map/all_to_all | solution.py:45
  293.2 14.2 %copy-start.5 = (f32[512]{0:T(512)S(1)}, f32[512]{0:T(512)}, u32[]{:S(2)}) copy-start(f32[512]{0:T(512)} %param.17) | copy-start | bytes 6148
Sparse Core Ops, SparseCore 0:
  11.3 58.2 all-reduce.1
  203.7 38.5 all-gather.1
where the time goes:
time: 317 us; the launch traced here: 316 us
  waiting for transfers between devices  123 us (39%)
  blocking collectives  121 us (38%)
  local copies, waits for them, and re-layouts  28.7 us (9%)
  starting transfers between devices  14.7 us (5%)
  between operations  13.6 us (4%)
  matrix products  9.02 us (3%)
  other arithmetic  6.31 us (2%)
    all_to_all x1, blocking collectives, body(): lax.all_to_all(outgoing, 'req', split_axis=0, concat_axis=0, tiled=True)  111 us
    psum x1, waiting for transfers between devices, body(): projected = lax.psum(partial_value, 'tp')  53.9 us
    all_gather x1, waiting for transfers between devices, body(): lax.all_gather(hidden, 'tp', axis=1, tiled=True)  38.7 us
    all_to_all x1, waiting for transfers between devices, body(): lax.all_to_all(expert_out, 'req', split_axis=0, concat_axis=0, tiled=True)  30.2 us
    all_to_all x1, starting transfers between devices, body(): lax.all_to_all(expert_out, 'req', split_axis=0, concat_axis=0, tiled=True)  14.6 us
    psum x1, blocking collectives, body(): square_total = lax.psum(square_part, 'tp')  9.8 us
  transfers between devices with their start and end apart: 3, of which 3 were waited for; matrix products, arithmetic and copies ran while one was open for 2% of the time, Pallas kernels for 0%

commit v1 on v0

v1 whole, which is shorter than its diff:
```python
import functools

import jax
import jax.numpy as jnp
from jax import lax
from jax.experimental import pallas as pl
from jax.experimental.pallas import tpu as pltpu
from jax.sharding import PartitionSpec as P

NY, NZ, NC, NX = 8, 8, 2, 4
CAP = 6
PAIR = NC * CAP
F32, BF16 = jnp.float32, jnp.bfloat16
MESH = pl.DeviceIdType.MESH


def dot(a, b):
    return jnp.dot(a, b, preferred_element_type=F32)


def dot_rows(a, b):
    return lax.dot_general(a, b, (((0,), (0,)), ((), ())), preferred_element_type=F32)


def step_of(k):
    return (2 * (k % 2) - 1) * ((k + 1) // 2)


def kernel(
    attn, w_out, resid, meta, w_gate, w_up, w_down, gain, out,
    wo, wgu, wd, part, part32, rs_in, proj, meta_all, pick, comb_hi, comb_lo,
    rows, zsend, feat, hid, oexp, back, acc, ysend, yin, ss_own, ss_in,
    load_sem, meta_s, meta_r, rs_s, rs_r, yag_s, yag_r, z_s, z_r,
    xa_s, xa_r, xf_s, xf_r, ha_s, ha_r, hf_s, hf_r, b_s, b_r, yr_s, yr_r, ss_s, ss_r,
):
    nrow, width = attn.shape
    full = w_out.shape[1]
    chunk = NY * PAIR
    half = chunk // 2
    hw = w_gate.shape[1]
    req, x = lax.axis_index("req"), lax.axis_index("tp")
    c = req % NC
    z = (req // NC) % NZ
    y = req // (NC * NZ)

    def at_x(d):
        return {"tp": (x + d + NX) % NX}

    def at_y(d):
        return {"req": (((y + d + NY) % NY) * NZ + z) * NC + c}

    def at_z(d):
        return {"req": (y * NZ + (z + d + NZ) % NZ) * NC + c}

    def remote(src, dst, s, r, dev):
        return pltpu.make_async_remote_copy(
            src_ref=src, dst_ref=dst, send_sem=s, recv_sem=r, device_id=dev, device_id_type=MESH
        )

    loads = [
        pltpu.make_async_copy(w_out, wo, load_sem.at[0]),
        pltpu.make_async_copy(w_gate, wgu.at[:, :hw], load_sem.at[1]),
        pltpu.make_async_copy(w_up, wgu.at[:, hw:], load_sem.at[2]),
        pltpu.make_async_copy(w_down, wd, load_sem.at[3]),
    ]
    for load in loads:
        load.start()

    barrier = pltpu.get_barrier_semaphore()
    partners = [at_x(d) for d in range(1, NX)]
    partners += [at_y(d) for d in range(1, NY)]
    partners += [at_z(d) for d in range(1, NZ)]
    for dev in partners:
        pl.semaphore_signal(barrier, inc=1, device_id=dev, device_id_type=MESH)

    loads[0].wait()
    for q in range(NX):
        value = dot(attn[...], wo[:, q * width:(q + 1) * width])
        part32[q] = value
        part[q] = value.astype(BF16)
    meta_all[y] = meta[...]
    pl.semaphore_wait(barrier, len(partners))

    meta_copies, rs_copies = [], []
    for d in range(1, NY):
        copy = remote(meta, meta_all.at[y], meta_s.at[d - 1], meta_r.at[d - 1], at_y(d))
        copy.start()
        meta_copies.append(copy)
    for d in range(1, NX):
        copy = remote(part.at[(x + d) % NX], rs_in.at[d - 1], rs_s.at[d - 1], rs_r.at[d - 1], at_x(d))
        copy.start()
        rs_copies.append(copy)

    for d in range(1, NY):
        remote(
            meta, meta_all.at[(y - d + NY) % NY], meta_s.at[d - 1], meta_r.at[d - 1], at_y(d)
        ).wait_recv()
    lanes = 2 * nrow
    place = lax.broadcasted_iota(jnp.int32, (chunk, lanes), 0)
    lane = lax.broadcasted_iota(jnp.int32, (chunk, lanes), 1)
    place_y, place_c, place_p = place // PAIR, (place // CAP) % NC, place % CAP
    before = lax.broadcasted_iota(jnp.int32, (lanes, lanes), 0)
    after = lax.broadcasted_iota(jnp.int32, (lanes, lanes), 1)
    earlier = ((before < after) & (before // nrow == after // nrow)).astype(F32).astype(BF16)

    def plan(zz, carry):
        slot = ((y * NZ + zz) * NC + place_c).astype(F32)
        for j in range(NY // 2):
            both = meta_all[2 * j] + meta_all[2 * j + 1]
            mine = place_y == 2 * j + lane // nrow
            hit = jnp.zeros((chunk, lanes), F32)
            gate = jnp.zeros((chunk, lanes), F32)
            for k in range(6):
                same = mine & (both[k:k + 1, :] == slot)
                hit = jnp.where(same, 1.0, hit)
                gate = jnp.where(same, both[8 + k:9 + k, :], gate)
            rank = dot(hit.astype(BF16), earlier)
            chosen = (hit > 0.0) & (rank == place_p.astype(F32))
            here = pl.ds(j * lanes, lanes)
            pick[zz, :, here] = jnp.where(chosen, 1.0, 0.0).astype(BF16)
            gate = jnp.where(chosen, gate, 0.0)
            high = gate.astype(BF16)
            comb_hi[zz, :, here] = high
            comb_lo[zz, :, here] = (gate - high.astype(F32)).astype(BF16)
        return carry

    lax.fori_loop(0, NZ, plan, 0)

    own = part32[x] + resid[...].astype(F32)
    for d in range(1, NX):
        remote(part.at[0], rs_in.at[d - 1], rs_s.at[d - 1], rs_r.at[d - 1], at_x(d)).wait_recv()
        own = own + rs_in[d - 1].astype(F32)
    proj[...] = own
    rows[y] = own.astype(BF16)

    yag = []
    for s in range(1, NY // 2 + 1):
        cut = s == NY // 2
        right = rows.at[(y - s + 1 + NY) % NY]
        left = rows.at[(y + s - 1) % NY]
        if s > 1:
            remote(right, right, yag_s.at[0, s - 2], yag_r.at[0, s - 2], at_y(-1)).wait_recv()
            remote(left, left, yag_s.at[1, s - 2], yag_r.at[1, s - 2], at_y(1)).wait_recv()
        if cut:
            right, left = right.at[:nrow // 2], left.at[nrow // 2:]
        one = remote(right, right, yag_s.at[0, s - 1], yag_r.at[0, s - 1], at_y(1))
        two = remote(left, left, yag_s.at[1, s - 1], yag_r.at[1, s - 1], at_y(-1))
        one.start()
        two.start()
        yag += [one, two]
    far = rows.at[(y + NY // 2) % NY]
    remote(far.at[:nrow // 2], far.at[:nrow // 2], yag_s.at[0, NY // 2 - 1], yag_r.at[0, NY // 2 - 1], at_y(-1)).wait_recv()
    remote(far.at[nrow // 2:], far.at[nrow // 2:], yag_s.at[1, NY // 2 - 1], yag_r.at[1, NY // 2 - 1], at_y(1)).wait_recv()

    def source_of(k):
        return (z - step_of(k) + NZ) % NZ

    def xa(k, right):
        block = feat.at[x, source_of(k)]
        i = 0 if right else 1
        return remote(block, block, xa_s.at[k, i], xa_r.at[k, i], at_x(1 if right else -1))

    def xf(k, right):
        n = source_of(k)
        i = 0 if right else 1
        rng = pl.ds(0, half) if right else pl.ds(half, half)
        block = feat.at[(x + NX - 1) % NX if right else (x + 1) % NX, n, rng]
        return remote(block, block, xf_s.at[k, i], xf_r.at[k, i], at_x(1 if right else -1))

    def ha(k, right):
        block = hid.at[x, source_of(k)]
        i = 0 if right else 1
        return remote(block, block, ha_s.at[k, i], ha_r.at[k, i], at_x(1 if right else -1))

    def hf(k, right):
        n = source_of(k)
        i = 0 if right else 1
        rng = pl.ds(0, half) if right else pl.ds(half, half)
        block = hid.at[(x + NX - 1) % NX if right else (x + 1) % NX, n, rng]
        return remote(block, block, hf_s.at[k, i], hf_r.at[k, i], at_x(1 if right else -1))

    def zsend_copy(k):
        n = (z + step_of(k) + NZ) % NZ
        return remote(zsend.at[n], feat.at[x, z], z_s.at[k], z_r.at[k], at_z(step_of(k)))

    def zback_copy(k):
        n = source_of(k)
        return remote(oexp.at[n], back.at[z], b_s.at[k], b_r.at[k], at_z(-step_of(k)))

    all_rows = rows[...].reshape(NY * nrow, width)
    feat[x, z] = dot(pick[z], all_rows).astype(BF16)
    xa(0, True).start()
    xa(0, False).start()

    def scatter(k, carry):
        n = (z + step_of(k) + NZ) % NZ
        zsend[n] = dot(pick[n], rows[...].reshape(NY * nrow, width)).astype(BF16)
        zsend_copy(k).start()
        return carry

    lax.fori_loop(1, NZ, scatter, 0)
    for load in loads[1:]:
        load.wait()

    def stage(i, carry):
        @pl.when((i >= 1) & (i < NZ))
        def _():
            n = source_of(i)
            remote(zsend.at[n], feat.at[x, n], z_s.at[i], z_r.at[i], at_z(step_of(i))).wait_recv()
            xa(i, True).start()
            xa(i, False).start()

        @pl.when((i >= 1) & (i < NZ + 1))
        def _():
            k = i - 1
            n = source_of(k)
            left, right = feat.at[(x + NX - 1) % NX, n], feat.at[(x + 1) % NX, n]
            remote(left, left, xa_s.at[k, 0], xa_r.at[k, 0], at_x(-1)).wait_recv()
            xf(k, True).start()
            remote(right, right, xa_s.at[k, 1], xa_r.at[k, 1], at_x(1)).wait_recv()
            xf(k, False).start()

        @pl.when((i >= 2) & (i < NZ + 2))
        def _():
            k = i - 2
            n = source_of(k)
            far = feat.at[(x + 2) % NX, n]
            low, high = far.at[pl.ds(0, half)], far.at[pl.ds(half, half)]
            remote(low, low, xf_s.at[k, 0], xf_r.at[k, 0], at_x(-1)).wait_recv()
            remote(high, high, xf_s.at[k, 1], xf_r.at[k, 1], at_x(1)).wait_recv()
            both = dot(feat[0, n], wgu[0:width, :])
            for q in range(1, NX):
                both = both + dot(feat[q, n], wgu[q * width:(q + 1) * width, :])
            gate, up = both[:, :hw], both[:, hw:]
            hid[x, n] = (gate / (1.0 + jnp.exp(-gate)) * up).astype(BF16)
            ha(k, True).start()
            ha(k, False).start()

        @pl.when((i >= 3) & (i < NZ + 3))
        def _():
            k = i - 3
            n = source_of(k)
            left, right = hid.at[(x + NX - 1) % NX, n], hid.at[(x + 1) % NX, n]
            remote(left, left, ha_s.at[k, 0], ha_r.at[k, 0], at_x(-1)).wait_recv()
            hf(k, True).start()
            remote(right, right, ha_s.at[k, 1], ha_r.at[k, 1], at_x(1)).wait_recv()
            hf(k, False).start()

        @pl.when(i >= 4)
        def _():
            k = i - 4
            n = source_of(k)
            far = hid.at[(x + 2) % NX, n]
            low, high = far.at[pl.ds(0, half)], far.at[pl.ds(half, half)]
            remote(low, low, hf_s.at[k, 0], hf_r.at[k, 0], at_x(-1)).wait_recv()
            remote(high, high, hf_s.at[k, 1], hf_r.at[k, 1], at_x(1)).wait_recv()
            value = dot(hid[0, n], wd[0:hw, :])
            for q in range(1, NX):
                value = value + dot(hid[q, n], wd[q * hw:(q + 1) * hw, :])

            @pl.when(k == 0)
            def _():
                back[z] = value.astype(BF16)

            @pl.when(k > 0)
            def _():
                oexp[n] = value.astype(BF16)
                zback_copy(k).start()

        return carry

    lax.fori_loop(0, NZ + 4, stage, 0)

    def gather(k, carry):
        n = (z + step_of(k) + NZ) % NZ

        @pl.when(k > 0)
        def _():
            remote(oexp.at[n], back.at[n], b_s.at[k], b_r.at[k], at_z(step_of(k))).wait_recv()

        value = dot_rows(comb_hi[n], back[n]) + dot_rows(comb_lo[n], back[n])

        @pl.when(k == 0)
        def _():
            acc[...] = value

        @pl.when(k > 0)
        def _():
            acc[...] += value

        return carry

    lax.fori_loop(0, NZ, gather, 0)
    for q in range(NY):
        ysend[q] = acc[q * nrow:(q + 1) * nrow, :].astype(BF16)
    yr = []
    for d in (4, 3, 5, 2, 6, 1, 7):
        copy = remote(ysend.at[(y + d) % NY], yin.at[d - 1], yr_s.at[d - 1], yr_r.at[d - 1], at_y(d))
        copy.start()
        yr.append(copy)
    total = proj[...] + acc[pl.ds(pl.multiple_of(y * nrow, nrow), nrow), :]
    for d in range(1, NY):
        remote(ysend.at[0], yin.at[d - 1], yr_s.at[d - 1], yr_r.at[d - 1], at_y(d)).wait_recv()
        total = total + yin[d - 1].astype(F32)

    square = jnp.sum(total * total, axis=1, keepdims=True)
    ss_own[...] = jnp.broadcast_to(square, ss_own.shape)
    ss = []
    for d in range(1, NX):
        copy = remote(ss_own, ss_in.at[d - 1], ss_s.at[d - 1], ss_r.at[d - 1], at_x(d))
        copy.start()
        ss.append(copy)
    for d in range(1, NX):
        remote(ss_own, ss_in.at[d - 1], ss_s.at[d - 1], ss_r.at[d - 1], at_x(d)).wait_recv()
        square = square + ss_in[d - 1][:, 0:1]
    scale = lax.rsqrt(square / full + 1e-06)
    out[...] = (total * scale * gain[...]).astype(BF16)

    for copy in meta_copies + rs_copies + yag + yr + ss:
        copy.wait_send()

    def drain(k, carry):
        for make in (xa, xf, ha, hf):
            make(k, True).wait_send()
            make(k, False).wait_send()

        @pl.when(k > 0)
        def _():
            zsend_copy(k).wait_send()
            zback_copy(k).wait_send()

        return carry

    lax.fori_loop(0, NZ, drain, 0)


def body(attn_out, w_out, residual, routes, gates, w_gate, w_up, w_down, norm_gain):
    nrow, width = attn_out.shape
    full = w_out.shape[1]
    topk = routes.shape[1]
    hw = w_gate.shape[2]
    chunk = NY * PAIR
    y = lax.axis_index("req") // (NC * NZ)
    pad = ((0, 8 - topk), (0, 0))
    tile = jnp.concatenate(
        [jnp.pad(routes.T.astype(F32), pad), jnp.pad(gates.T.astype(F32), pad)], axis=0
    )
    odd = y % 2 == 1
    meta = jnp.concatenate([jnp.where(odd, 0.0, tile), jnp.where(odd, tile, 0.0)], axis=1)
    vmem = pl.BlockSpec(memory_space=pltpu.VMEM)
    anyw = pl.BlockSpec(memory_space=pl.ANY)
    dma = pltpu.SemaphoreType.DMA
    scratch = [
        pltpu.VMEM((width, full), BF16),
        pltpu.VMEM((full, 2 * hw), BF16),
        pltpu.VMEM((NX * hw, width), BF16),
        pltpu.VMEM((NX, nrow, width), BF16),
        pltpu.VMEM((NX, nrow, width), F32),
        pltpu.VMEM((NX - 1, nrow, width), BF16),
        pltpu.VMEM((nrow, width), F32),
        pltpu.VMEM((NY, 16, 2 * nrow), F32),
        pltpu.VMEM((NZ, chunk, NY * nrow), BF16),
        pltpu.VMEM((NZ, chunk, NY * nrow), BF16),
        pltpu.VMEM((NZ, chunk, NY * nrow), BF16),
        pltpu.VMEM((NY, nrow, width), BF16),
        pltpu.VMEM((NZ, chunk, width), BF16),
        pltpu.VMEM((NX, NZ, chunk, width), BF16),
        pltpu.VMEM((NX, NZ, chunk, hw), BF16),
        pltpu.VMEM((NZ, chunk, width), BF16),
        pltpu.VMEM((NZ, chunk, width), BF16),
        pltpu.VMEM((NY * nrow, width), F32),
        pltpu.VMEM((NY, nrow, width), BF16),
        pltpu.VMEM((NY - 1, nrow, width), BF16),
        pltpu.VMEM((nrow, 128), F32),
        pltpu.VMEM((NX - 1, nrow, 128), F32),
        dma((4,)),
        dma((NY - 1,)), dma((NY - 1,)),
        dma((NX - 1,)), dma((NX - 1,)),
        dma((2, NY // 2)), dma((2, NY // 2)),
        dma((NZ,)), dma((NZ,)),
        dma((NZ, 2)), dma((NZ, 2)),
        dma((NZ, 2)), dma((NZ, 2)),
        dma((NZ, 2)), dma((NZ, 2)),
        dma((NZ, 2)), dma((NZ, 2)),
        dma((NZ,)), dma((NZ,)),
        dma((NY - 1,)), dma((NY - 1,)),
        dma((NX - 1,)), dma((NX - 1,)),
    ]
    return pl.pallas_call(
        kernel,
        out_shape=jax.ShapeDtypeStruct((nrow, width), BF16),
        in_specs=[vmem, anyw, vmem, vmem, anyw, anyw, anyw, vmem],
        out_specs=vmem,
        scratch_shapes=scratch,
        compiler_params=pltpu.CompilerParams(collective_id=0, has_side_effects=True),
    )(attn_out, w_out, residual, meta, w_gate[0], w_up[0], w_down[0], norm_gain[None, :])


def solution(mesh):
    placed = (
        P("req", "tp"),
        P("tp", None),
        P("req", "tp"),
        P("req", None),
        P("req", None),
        P("req", None, "tp"),
        P("req", None, "tp"),
        P("req", None, "tp"),
        P("tp"),
    )
    return jax.shard_map(
        body, mesh=mesh, in_specs=placed, out_specs=P("req", "tp"), check_vma=False
    )
```

time: 317 us -> 113 us (0.36)
  waiting for transfers between devices: 123 us -> 0 us
  blocking collectives: 121 us -> 0 us
  Pallas kernels: 0 us -> 109 us
  local copies, waits for them, and re-layouts: 28.7 us -> 1.47 us
  starting transfers between devices: 14.7 us -> 0 us
  between operations: 13.6 us -> 0.01 us
  matrix products: 9.02 us -> 0 us
  other arithmetic: 6.31 us -> 2.06 us
    all_to_all x1 -> x0, blocking collectives: 111 us -> none  [body(): lax.all_to_all(outgoing, 'req', split_axis=0, concat_axis=0, tiled=True)]
    pallas_call x0 -> x1, Pallas kernels: none -> 109 us  [body(): pl.pallas_call(kernel, out_shape=jax.ShapeDtypeStruct((nrow, width), BF16...]
    psum x1 -> x0, waiting for transfers between devices: 53.9 us -> none  [body(): projected = lax.psum(partial_value, 'tp')]
    all_gather x1 -> x0, waiting for transfers between devices: 38.7 us -> none  [body(): lax.all_gather(hidden, 'tp', axis=1, tiled=True)]
    all_to_all x1 -> x0, waiting for transfers between devices: 30.2 us -> none  [body(): lax.all_to_all(expert_out, 'req', split_axis=0, concat_axis=0, tiled=True)]
    reshape x5 -> x0, local copies, waits for them, and re-layouts: 15.4 us -> none  [the longest x1 6.34 us: body(): expert_rows = incoming.reshape(slot_count * capacity, full_width)]
    all_to_all x1 -> x0, starting transfers between devices: 14.6 us -> none  [body(): lax.all_to_all(expert_out, 'req', split_axis=0, concat_axis=0, tiled=True)]
    psum x1 -> x0, blocking collectives: 9.8 us -> none  [body(): square_total = lax.psum(square_part, 'tp')]
  transfers between devices with their start and end apart: 3 -> 0, of which waited for: 3 -> 0; matrix products, arithmetic and copies ran while one was open for 2% -> 0% of each run, Pallas kernels for 0% -> 0%
where the time goes in v1:
time: 113 us
  Pallas kernels  109 us (96%)
  other arithmetic  2.06 us (2%)
  local copies, waits for them, and re-layouts  1.47 us (1%)
    pallas_call x1, Pallas kernels, body(): pl.pallas_call(kernel, out_shape=jax.ShapeDtypeStruct((nrow, width), BF16...  109 us

profile of v1, /device:TPU:8, one launch (start us, length us, event | category | flops | bytes accessed | tf_op | source)
XLA Modules:
  0.0 112.7 jit_solution(11093362494249257055)
XLA Ops:
  0.0 0.7 convert_bitcast_fusion
  0.7 0.7 fusion.1
  1.4 0.7 pad_maximum_fusion.meta
  2.1 109.1 %shard_map.91 = bf16[64,512]{1,0:T(8,128)(2,1)} custom-call(bf16[64,512]{1,0:T(8,128)(2,1)} %attn.1, bf16[512,2048]{1,0:T(8,128)(2,1)} %w_out.1, bf16[64,512]{1,0:T(8,128)(2,1)} %resid.1, f32[16,128]{1,0:T(8,128)} %pad_maximum_fusion.meta, bf16[2048,256]{1,0:T(8,128)(2,1)} %bitcast.7, bf16[2048,256]{1,0:T(8,128)(2,1)} %bitcast.8, bf16[1024,512]{1,0:T(8,128)(2,1)} %bitcast.9, ...), custom_call_target="tpu_custom_call" | custom-call | tf_op jit(solution)/shard_map/pallas_call | solution.py:389
  111.2 1.5 %copy.11 = bf16[64,512]{1,0:T(8,128)(2,1)} copy(bf16[64,512]{1,0:T(8,128)(2,1)} %shard_map.91) | data formatting | bytes 131072

commit v2 on v1

--- a/solution.py
+++ b/solution.py
@@ -40,17 +40,22 @@
     hw = w_gate.shape[1]
     req, x = lax.axis_index("req"), lax.axis_index("tp")
     c = req % NC
-    z = (req // NC) % NZ
-    y = req // (NC * NZ)
+    pz = (req // NC) % NZ
+    py = req // (NC * NZ)
+    y = py + c * (pz - py)
+    z = pz + c * (py - pz)
 
     def at_x(d):
         return {"tp": (x + d + NX) % NX}
 
+    def chip(yy, zz):
+        return yy * (NZ + c * (1 - NZ)) + zz * (1 + c * (NZ - 1))
+
     def at_y(d):
-        return {"req": (((y + d + NY) % NY) * NZ + z) * NC + c}
+        return {"req": chip((y + d + NY) % NY, z) * NC + c}
 
     def at_z(d):
-        return {"req": (y * NZ + (z + d + NZ) % NZ) * NC + c}
+        return {"req": chip(y, (z + d + NZ) % NZ) * NC + c}
 
     def remote(src, dst, s, r, dev):
         return pltpu.make_async_remote_copy(
@@ -104,7 +109,7 @@
     earlier = ((before < after) & (before // nrow == after // nrow)).astype(F32).astype(BF16)
 
     def plan(zz, carry):
-        slot = ((y * NZ + zz) * NC + place_c).astype(F32)
+        slot = (chip(y, zz) * NC + place_c).astype(F32)
         for j in range(NY // 2):
             both = meta_all[2 * j] + meta_all[2 * j + 1]
             mine = place_y == 2 * j + lane // nrow
@@ -134,23 +139,13 @@
     rows[y] = own.astype(BF16)
 
     yag = []
-    for s in range(1, NY // 2 + 1):
-        cut = s == NY // 2
-        right = rows.at[(y - s + 1 + NY) % NY]
-        left = rows.at[(y + s - 1) % NY]
-        if s > 1:
-            remote(right, right, yag_s.at[0, s - 2], yag_r.at[0, s - 2], at_y(-1)).wait_recv()
-            remote(left, left, yag_s.at[1, s - 2], yag_r.at[1, s - 2], at_y(1)).wait_recv()
-        if cut:
-            right, left = right.at[:nrow // 2], left.at[nrow // 2:]
-        one = remote(right, right, yag_s.at[0, s - 1], yag_r.at[0, s - 1], at_y(1))
-        two = remote(left, left, yag_s.at[1, s - 1], yag_r.at[1, s - 1], at_y(-1))
-        one.start()
-        two.start()
-        yag += [one, two]
-    far = rows.at[(y + NY // 2) % NY]
-    remote(far.at[:nrow // 2], far.at[:nrow // 2], yag_s.at[0, NY // 2 - 1], yag_r.at[0, NY // 2 - 1], at_y(-1)).wait_recv()
-    remote(far.at[nrow // 2:], far.at[nrow // 2:], yag_s.at[1, NY // 2 - 1], yag_r.at[1, NY // 2 - 1], at_y(1)).wait_recv()
+    for d in (4, 3, 5, 2, 6, 1, 7):
+        copy = remote(rows.at[y], rows.at[y], yag_s.at[d - 1], yag_r.at[d - 1], at_y(d))
+        copy.start()
+        yag.append(copy)
+    for d in (1, 7, 2, 6, 3, 5, 4):
+        block = rows.at[(y - d + NY) % NY]
+        remote(block, block, yag_s.at[d - 1], yag_r.at[d - 1], at_y(-d)).wait_recv()
 
     def source_of(k):
         return (z - step_of(k) + NZ) % NZ
@@ -340,7 +335,9 @@
     topk = routes.shape[1]
     hw = w_gate.shape[2]
     chunk = NY * PAIR
-    y = lax.axis_index("req") // (NC * NZ)
+    req = lax.axis_index("req")
+    y, z = req // (NC * NZ), (req // NC) % NZ
+    y = jnp.where(req % NC == 1, z, y)
     pad = ((0, 8 - topk), (0, 0))
     tile = jnp.concatenate(
         [jnp.pad(routes.T.astype(F32), pad), jnp.pad(gates.T.astype(F32), pad)], axis=0
@@ -376,7 +373,7 @@
         dma((4,)),
         dma((NY - 1,)), dma((NY - 1,)),
         dma((NX - 1,)), dma((NX - 1,)),
-        dma((2, NY // 2)), dma((2, NY // 2)),
+        dma((NY - 1,)), dma((NY - 1,)),
         dma((NZ,)), dma((NZ,)),
         dma((NZ, 2)), dma((NZ, 2)),
         dma((NZ, 2)), dma((NZ, 2)),

time: 113 us -> 108 us (0.956)
  the two profiles are of different devices: /device:TPU:8 before, /device:TPU:2 now
where the time goes in v2:
time: 108 us
  Pallas kernels  104 us (96%)
  other arithmetic  2.06 us (2%)
  local copies, waits for them, and re-layouts  1.47 us (1%)
    pallas_call x1, Pallas kernels, body(): pl.pallas_call(kernel, out_shape=jax.ShapeDtypeStruct((nrow, width), BF16...  104 us

profile of v2, /device:TPU:2, one launch (start us, length us, event | category | flops | bytes accessed | tf_op | source)
XLA Modules:
  0.0 107.9 jit_solution(17488060459337042416)
XLA Ops:
  0.0 0.7 convert_bitcast_fusion
  0.7 0.7 fusion.1
  1.4 0.7 pad_maximum_fusion.meta
  2.1 104.4 %shard_map.91 = bf16[64,512]{1,0:T(8,128)(2,1)} custom-call(bf16[64,512]{1,0:T(8,128)(2,1)} %attn.1, bf16[512,2048]{1,0:T(8,128)(2,1)} %w_out.1, bf16[64,512]{1,0:T(8,128)(2,1)} %resid.1, f32[16,128]{1,0:T(8,128)} %pad_maximum_fusion.meta, bf16[2048,256]{1,0:T(8,128)(2,1)} %bitcast.7, bf16[2048,256]{1,0:T(8,128)(2,1)} %bitcast.8, bf16[1024,512]{1,0:T(8,128)(2,1)} %bitcast.9, ...), custom_call_target="tpu_custom_call" | custom-call | tf_op jit(solution)/shard_map/pallas_call | solution.py:386
  106.5 1.5 %copy.11 = bf16[64,512]{1,0:T(8,128)(2,1)} copy(bf16[64,512]{1,0:T(8,128)(2,1)} %shard_map.91) | data formatting | bytes 131072

commit v3 on v2

--- a/solution.py
+++ b/solution.py
@@ -22,12 +22,8 @@
     return lax.dot_general(a, b, (((0,), (0,)), ((), ())), preferred_element_type=F32)
 
 
-def step_of(k):
-    return (2 * (k % 2) - 1) * ((k + 1) // 2)
-
-
 def kernel(
-    attn, w_out, resid, meta, w_gate, w_up, w_down, gain, out,
+    attn, w_out, resid, routes, gates, w_gate, w_up, w_down, gain, out,
     wo, wgu, wd, part, part32, rs_in, proj, meta_all, pick, comb_hi, comb_lo,
     rows, zsend, feat, hid, oexp, back, acc, ysend, yin, ss_own, ss_in,
     load_sem, meta_s, meta_r, rs_s, rs_r, yag_s, yag_r, z_s, z_r,
@@ -62,44 +58,61 @@
             src_ref=src, dst_ref=dst, send_sem=s, recv_sem=r, device_id=dev, device_id_type=MESH
         )
 
+    barrier = pltpu.get_barrier_semaphore()
+    partners = [at_x(d) for d in range(1, NX)]
+    partners += [at_y(d) for d in range(1, NY)]
+    partners += [at_z(d) for d in range(1, NZ)]
+    for dev in partners:
+        pl.semaphore_signal(barrier, inc=1, device_id=dev, device_id_type=MESH)
+
     loads = [
         pltpu.make_async_copy(w_out, wo, load_sem.at[0]),
         pltpu.make_async_copy(w_gate, wgu.at[:, :hw], load_sem.at[1]),
         pltpu.make_async_copy(w_up, wgu.at[:, hw:], load_sem.at[2]),
         pltpu.make_async_copy(w_down, wd, load_sem.at[3]),
     ]
-    for load in loads:
+    loads[0].start()
+
+    odd = y % 2 == 1
+    nk = routes.shape[0]
+    meta_all[y] = jnp.zeros((16, 2 * nrow), F32)
+    for first, value in ((0, routes[...].astype(F32)), (8, gates[...])):
+        meta_all[y, first:first + nk, 0:nrow] = jnp.where(odd, 0.0, value)
+        meta_all[y, first:first + nk, nrow:2 * nrow] = jnp.where(odd, value, 0.0)
+    loads[0].wait()
+    for load in loads[1:]:
         load.start()
-
-    barrier = pltpu.get_barrier_semaphore()
-    partners = [at_x(d) for d in range(1, NX)]
-    partners += [at_y(d) for d in range(1, NY)]
-    partners += [at_z(d) for d in range(1, NZ)]
-    for dev in partners:
-        pl.semaphore_signal(barrier, inc=1, device_id=dev, device_id_type=MESH)
-
-    loads[0].wait()
     for q in range(NX):
         value = dot(attn[...], wo[:, q * width:(q + 1) * width])
         part32[q] = value
         part[q] = value.astype(BF16)
-    meta_all[y] = meta[...]
     pl.semaphore_wait(barrier, len(partners))
 
     meta_copies, rs_copies = [], []
+    for d in (2, 1, 3):
+        copy = remote(part.at[(x + d) % NX], rs_in.at[d - 1], rs_s.at[d - 1], rs_r.at[d - 1], at_x(d))
+        copy.start()
+        rs_copies.append(copy)
     for d in range(1, NY):
-        copy = remote(meta, meta_all.at[y], meta_s.at[d - 1], meta_r.at[d - 1], at_y(d))
+        copy = remote(meta_all.at[y], meta_all.at[y], meta_s.at[d - 1], meta_r.at[d - 1], at_y(d))
         copy.start()
         meta_copies.append(copy)
+
+    own = part32[x] + resid[...].astype(F32)
     for d in range(1, NX):
-        copy = remote(part.at[(x + d) % NX], rs_in.at[d - 1], rs_s.at[d - 1], rs_r.at[d - 1], at_x(d))
-        copy.start()
-        rs_copies.append(copy)
-
+        remote(part.at[0], rs_in.at[d - 1], rs_s.at[d - 1], rs_r.at[d - 1], at_x(d)).wait_recv()
+        own = own + rs_in[d - 1].astype(F32)
+    proj[...] = own
+    rows[y] = own.astype(BF16)
+
+    yag = []
+    for d in (4, 3, 5, 2, 6, 1, 7):
+        copy = remote(rows.at[y], rows.at[y], yag_s.at[d - 1], yag_r.at[d - 1], at_y(d))
+        copy.start()
+        yag.append(copy)
     for d in range(1, NY):
-        remote(
-            meta, meta_all.at[(y - d + NY) % NY], meta_s.at[d - 1], meta_r.at[d - 1], at_y(d)
-        ).wait_recv()
+        block = meta_all.at[(y - d + NY) % NY]
+        remote(block, block, meta_s.at[d - 1], meta_r.at[d - 1], at_y(d)).wait_recv()
     lanes = 2 * nrow
     place = lax.broadcasted_iota(jnp.int32, (chunk, lanes), 0)
     lane = lax.broadcasted_iota(jnp.int32, (chunk, lanes), 1)
@@ -131,24 +144,12 @@
 
     lax.fori_loop(0, NZ, plan, 0)
 
-    own = part32[x] + resid[...].astype(F32)
-    for d in range(1, NX):
-        remote(part.at[0], rs_in.at[d - 1], rs_s.at[d - 1], rs_r.at[d - 1], at_x(d)).wait_recv()
-        own = own + rs_in[d - 1].astype(F32)
-    proj[...] = own
-    rows[y] = own.astype(BF16)
-
-    yag = []
-    for d in (4, 3, 5, 2, 6, 1, 7):
-        copy = remote(rows.at[y], rows.at[y], yag_s.at[d - 1], yag_r.at[d - 1], at_y(d))
-        copy.start()
-        yag.append(copy)
     for d in (1, 7, 2, 6, 3, 5, 4):
         block = rows.at[(y - d + NY) % NY]
         remote(block, block, yag_s.at[d - 1], yag_r.at[d - 1], at_y(-d)).wait_recv()
 
     def source_of(k):
-        return (z - step_of(k) + NZ) % NZ
+        return (z - k + NZ) % NZ
 
     def xa(k, right):
         block = feat.at[x, source_of(k)]
@@ -175,12 +176,12 @@
         return remote(block, block, hf_s.at[k, i], hf_r.at[k, i], at_x(1 if right else -1))
 
     def zsend_copy(k):
-        n = (z + step_of(k) + NZ) % NZ
-        return remote(zsend.at[n], feat.at[x, z], z_s.at[k], z_r.at[k], at_z(step_of(k)))
+        n = (z + k + NZ) % NZ
+        return remote(zsend.at[n], feat.at[x, z], z_s.at[k], z_r.at[k], at_z(k))
 
     def zback_copy(k):
         n = source_of(k)
-        return remote(oexp.at[n], back.at[z], b_s.at[k], b_r.at[k], at_z(-step_of(k)))
+        return remote(oexp.at[n], back.at[z], b_s.at[k], b_r.at[k], at_z(-k))
 
     all_rows = rows[...].reshape(NY * nrow, width)
     feat[x, z] = dot(pick[z], all_rows).astype(BF16)
@@ -188,7 +189,7 @@
     xa(0, False).start()
 
     def scatter(k, carry):
-        n = (z + step_of(k) + NZ) % NZ
+        n = (z + k + NZ) % NZ
         zsend[n] = dot(pick[n], rows[...].reshape(NY * nrow, width)).astype(BF16)
         zsend_copy(k).start()
         return carry
@@ -201,7 +202,7 @@
         @pl.when((i >= 1) & (i < NZ))
         def _():
             n = source_of(i)
-            remote(zsend.at[n], feat.at[x, n], z_s.at[i], z_r.at[i], at_z(step_of(i))).wait_recv()
+            remote(zsend.at[n], feat.at[x, n], z_s.at[i], z_r.at[i], at_z(i)).wait_recv()
             xa(i, True).start()
             xa(i, False).start()
 
@@ -241,7 +242,7 @@
             remote(right, right, ha_s.at[k, 1], ha_r.at[k, 1], at_x(1)).wait_recv()
             hf(k, False).start()
 
-        @pl.when(i >= 4)
+        @pl.when((i >= 4) & (i < NZ + 4))
         def _():
             k = i - 4
             n = source_of(k)
@@ -262,30 +263,22 @@
                 oexp[n] = value.astype(BF16)
                 zback_copy(k).start()
 
+        @pl.when(i >= 6)
+        def _():
+            k = i - 6
+            n = (z + k) % NZ
+
+            @pl.when(k > 0)
+            def _():
+                remote(oexp.at[n], back.at[n], b_s.at[k], b_r.at[k], at_z(k)).wait_recv()
+
+            acc[...] += dot_rows(comb_hi[n], back[n]) + dot_rows(comb_lo[n], back[n])
+
         return carry
 
-    lax.fori_loop(0, NZ + 4, stage, 0)
-
-    def gather(k, carry):
-        n = (z + step_of(k) + NZ) % NZ
-
-        @pl.when(k > 0)
-        def _():
-            remote(oexp.at[n], back.at[n], b_s.at[k], b_r.at[k], at_z(step_of(k))).wait_recv()
-
-        value = dot_rows(comb_hi[n], back[n]) + dot_rows(comb_lo[n], back[n])
-
-        @pl.when(k == 0)
-        def _():
-            acc[...] = value
-
-        @pl.when(k > 0)
-        def _():
-            acc[...] += value
-
-        return carry
-
-    lax.fori_loop(0, NZ, gather, 0)
+    acc[...] = jnp.zeros(acc.shape, F32)
+    lax.fori_loop(0, NZ + 6, stage, 0)
+
     for q in range(NY):
         ysend[q] = acc[q * nrow:(q + 1) * nrow, :].astype(BF16)
     yr = []
@@ -332,18 +325,8 @@
 def body(attn_out, w_out, residual, routes, gates, w_gate, w_up, w_down, norm_gain):
     nrow, width = attn_out.shape
     full = w_out.shape[1]
-    topk = routes.shape[1]
     hw = w_gate.shape[2]
     chunk = NY * PAIR
-    req = lax.axis_index("req")
-    y, z = req // (NC * NZ), (req // NC) % NZ
-    y = jnp.where(req % NC == 1, z, y)
-    pad = ((0, 8 - topk), (0, 0))
-    tile = jnp.concatenate(
-        [jnp.pad(routes.T.astype(F32), pad), jnp.pad(gates.T.astype(F32), pad)], axis=0
-    )
-    odd = y % 2 == 1
-    meta = jnp.concatenate([jnp.where(odd, 0.0, tile), jnp.where(odd, tile, 0.0)], axis=1)
     vmem = pl.BlockSpec(memory_space=pltpu.VMEM)
     anyw = pl.BlockSpec(memory_space=pl.ANY)
     dma = pltpu.SemaphoreType.DMA
@@ -386,11 +369,11 @@
     return pl.pallas_call(
         kernel,
         out_shape=jax.ShapeDtypeStruct((nrow, width), BF16),
-        in_specs=[vmem, anyw, vmem, vmem, anyw, anyw, anyw, vmem],
+        in_specs=[vmem, anyw, vmem, vmem, vmem, anyw, anyw, anyw, vmem],
         out_specs=vmem,
         scratch_shapes=scratch,
         compiler_params=pltpu.CompilerParams(collective_id=0, has_side_effects=True),
-    )(attn_out, w_out, residual, meta, w_gate[0], w_up[0], w_down[0], norm_gain[None, :])
+    )(attn_out, w_out, residual, routes.T, gates.T, w_gate[0], w_up[0], w_down[0], norm_gain[None, :])
 
 
 def solution(mesh):

time: 108 us -> 102 us (0.944)
  the two profiles are of different devices: /device:TPU:2 before, /device:TPU:8 now
where the time goes in v3:
time: 102 us
  Pallas kernels  100 us (98%)
  local copies, waits for them, and re-layouts  1.47 us (1%)
    pallas_call x1, Pallas kernels, body(): pl.pallas_call(kernel, out_shape=jax.ShapeDtypeStruct((nrow, width), BF16...  100 us

profile of v3, /device:TPU:8, one launch (start us, length us, event | category | flops | bytes accessed | tf_op | source)
XLA Modules:
  0.0 101.8 jit_solution(5051782996364131399)
XLA Ops:
  0.0 100.3 %shard_map.91 = bf16[64,512]{1,0:T(8,128)(2,1)} custom-call(bf16[64,512]{1,0:T(8,128)(2,1)} %attn.1, bf16[512,2048]{1,0:T(8,128)(2,1)} %w_out.1, bf16[64,512]{1,0:T(8,128)(2,1)} %resid.1, s32[6,64]{1,0:T(8,128)} %bitcast.9, f32[6,64]{1,0:T(8,128)} %bitcast.10, bf16[2048,256]{1,0:T(8,128)(2,1)} %bitcast.6, bf16[2048,256]{1,0:T(8,128)(2,1)} %bitcast.7, ...), custom_call_target="tpu_custom_call" | custom-call | tf_op jit(solution)/shard_map/pallas_call | solution.py:369
  100.3 1.5 %copy.11 = bf16[64,512]{1,0:T(8,128)(2,1)} copy(bf16[64,512]{1,0:T(8,128)(2,1)} %shard_map.91) | data formatting | bytes 131072

commit v4 on v3

--- a/solution.py
+++ b/solution.py
@@ -229,12 +229,21 @@
                 both = both + dot(feat[q, n], wgu[q * width:(q + 1) * width, :])
             gate, up = both[:, :hw], both[:, hw:]
             hid[x, n] = (gate / (1.0 + jnp.exp(-gate)) * up).astype(BF16)
-            ha(k, True).start()
-            ha(k, False).start()
-
-        @pl.when((i >= 3) & (i < NZ + 3))
-        def _():
-            k = i - 3
+
+        @pl.when((i >= 5) & (i < NZ + 2))
+        def _():
+            ha(i - 5, True).start()
+            ha(i - 5, False).start()
+
+        @pl.when(i == NZ + 1)
+        def _():
+            for k in range(NZ - 3, NZ):
+                ha(k, True).start()
+                ha(k, False).start()
+
+        @pl.when((i >= 6) & (i < NZ + 6))
+        def _():
+            k = i - 6
             n = source_of(k)
             left, right = hid.at[(x + NX - 1) % NX, n], hid.at[(x + 1) % NX, n]
             remote(left, left, ha_s.at[k, 0], ha_r.at[k, 0], at_x(-1)).wait_recv()
@@ -242,9 +251,9 @@
             remote(right, right, ha_s.at[k, 1], ha_r.at[k, 1], at_x(1)).wait_recv()
             hf(k, False).start()
 
-        @pl.when((i >= 4) & (i < NZ + 4))
-        def _():
-            k = i - 4
+        @pl.when((i >= 7) & (i < NZ + 7))
+        def _():
+            k = i - 7
             n = source_of(k)
             far = hid.at[(x + 2) % NX, n]
             low, high = far.at[pl.ds(0, half)], far.at[pl.ds(half, half)]
@@ -263,9 +272,9 @@
                 oexp[n] = value.astype(BF16)
                 zback_copy(k).start()
 
-        @pl.when(i >= 6)
-        def _():
-            k = i - 6
+        @pl.when(i >= 9)
+        def _():
+            k = i - 9
             n = (z + k) % NZ
 
             @pl.when(k > 0)
@@ -277,7 +286,7 @@
         return carry
 
     acc[...] = jnp.zeros(acc.shape, F32)
-    lax.fori_loop(0, NZ + 6, stage, 0)
+    lax.fori_loop(0, NZ + 9, stage, 0)
 
     for q in range(NY):
         ysend[q] = acc[q * nrow:(q + 1) * nrow, :].astype(BF16)

time: 102 us -> 108 us (1.059)
  Pallas kernels: 100 us -> 106 us
    pallas_call x1, Pallas kernels: 100 us -> 106 us  [body(): pl.pallas_call(kernel, out_shape=jax.ShapeDtypeStruct((nrow, width), BF16...]
where the time goes in v4:
time: 108 us
  Pallas kernels  106 us (98%)
  local copies, waits for them, and re-layouts  1.47 us (1%)
    pallas_call x1, Pallas kernels, body(): pl.pallas_call(kernel, out_shape=jax.ShapeDtypeStruct((nrow, width), BF16...  106 us

profile of v4, /device:TPU:8, one launch (start us, length us, event | category | flops | bytes accessed | tf_op | source)
XLA Modules:
  0.0 107.7 jit_solution(17409143171615327211)
XLA Ops:
  0.0 106.2 %shard_map.91 = bf16[64,512]{1,0:T(8,128)(2,1)} custom-call(bf16[64,512]{1,0:T(8,128)(2,1)} %attn.1, bf16[512,2048]{1,0:T(8,128)(2,1)} %w_out.1, bf16[64,512]{1,0:T(8,128)(2,1)} %resid.1, s32[6,64]{1,0:T(8,128)} %bitcast.9, f32[6,64]{1,0:T(8,128)} %bitcast.10, bf16[2048,256]{1,0:T(8,128)(2,1)} %bitcast.6, bf16[2048,256]{1,0:T(8,128)(2,1)} %bitcast.7, ...), custom_call_target="tpu_custom_call" | custom-call | tf_op jit(solution)/shard_map/pallas_call | solution.py:378
  106.2 1.5 %copy.11 = bf16[64,512]{1,0:T(8,128)(2,1)} copy(bf16[64,512]{1,0:T(8,128)(2,1)} %shard_map.91) | data formatting | bytes 131072

commit v5 on v3

--- a/solution.py
+++ b/solution.py
@@ -10,6 +10,7 @@
 NY, NZ, NC, NX = 8, 8, 2, 4
 CAP = 6
 PAIR = NC * CAP
+TILE = 16
 F32, BF16 = jnp.float32, jnp.bfloat16
 MESH = pl.DeviceIdType.MESH
 
@@ -24,7 +25,7 @@
 
 def kernel(
     attn, w_out, resid, routes, gates, w_gate, w_up, w_down, gain, out,
-    wo, wgu, wd, part, part32, rs_in, proj, meta_all, pick, comb_hi, comb_lo,
+    wo, wgu, wd, part, part32, rs_in, proj, meta_all, pick, comb_hi, comb_lo, spread,
     rows, zsend, feat, hid, oexp, back, acc, ysend, yin, ss_own, ss_in,
     load_sem, meta_s, meta_r, rs_s, rs_r, yag_s, yag_r, z_s, z_r,
     xa_s, xa_r, xf_s, xf_r, ha_s, ha_r, hf_s, hf_r, b_s, b_r, yr_s, yr_r, ss_s, ss_r,
@@ -127,22 +128,45 @@
             both = meta_all[2 * j] + meta_all[2 * j + 1]
             mine = place_y == 2 * j + lane // nrow
             hit = jnp.zeros((chunk, lanes), F32)
-            gate = jnp.zeros((chunk, lanes), F32)
-            for k in range(6):
-                same = mine & (both[k:k + 1, :] == slot)
-                hit = jnp.where(same, 1.0, hit)
-                gate = jnp.where(same, both[8 + k:9 + k, :], gate)
+            for k in range(nk):
+                hit = jnp.where(both[k:k + 1, :] == slot, 1.0, hit)
+            hit = jnp.where(mine, hit, 0.0)
             rank = dot(hit.astype(BF16), earlier)
             chosen = (hit > 0.0) & (rank == place_p.astype(F32))
             here = pl.ds(j * lanes, lanes)
             pick[zz, :, here] = jnp.where(chosen, 1.0, 0.0).astype(BF16)
-            gate = jnp.where(chosen, gate, 0.0)
-            high = gate.astype(BF16)
-            comb_hi[zz, :, here] = high
-            comb_lo[zz, :, here] = (gate - high.astype(F32)).astype(BF16)
         return carry
 
     lax.fori_loop(0, NZ, plan, 0)
+
+    line = lax.broadcasted_iota(jnp.int32, (NY * TILE, lanes), 0)
+    in_y, in_q = line // TILE, line % TILE
+    mine_home = (lax.broadcasted_iota(jnp.int32, line.shape, 1) // nrow == y % 2) & (in_q < PAIR)
+
+    def plan_home(zz, carry):
+        slot = (chip(in_y, zz) * NC + in_q // CAP).astype(F32)
+        own = meta_all[y]
+        hit = jnp.zeros(line.shape, F32)
+        gate = jnp.zeros(line.shape, F32)
+        for k in range(nk):
+            same = own[k:k + 1, :] == slot
+            hit = jnp.where(same, 1.0, hit)
+            gate = jnp.where(same, own[8 + k:9 + k, :], gate)
+        hit = jnp.where(mine_home, hit, 0.0)
+        rank = dot(hit.astype(BF16), earlier)
+        chosen = (hit > 0.0) & (rank == (in_q % CAP).astype(F32))
+        gate = jnp.where(chosen, gate, 0.0)
+        high = gate.astype(BF16)
+        comb_hi[zz] = high
+        comb_lo[zz] = (gate - high.astype(F32)).astype(BF16)
+        return carry
+
+    lax.fori_loop(0, NZ, plan_home, 0)
+    to = lax.broadcasted_iota(jnp.int32, spread.shape, 0)
+    of = lax.broadcasted_iota(jnp.int32, spread.shape, 1)
+    moved = (to // TILE == of // PAIR) & (to % TILE == of % PAIR)
+    spread[...] = jnp.where(moved, 1.0, 0.0).astype(BF16)
+    acc[...] = jnp.zeros(acc.shape, F32)
 
     for d in (1, 7, 2, 6, 3, 5, 4):
         block = rows.at[(y - d + NY) % NY]
@@ -178,6 +202,10 @@
     def zsend_copy(k):
         n = (z + k + NZ) % NZ
         return remote(zsend.at[n], feat.at[x, z], z_s.at[k], z_r.at[k], at_z(k))
+
+    def yr(k, d):
+        n = (z + k) % NZ
+        return remote(ysend.at[n, (y + d) % NY], yin.at[n, y], yr_s.at[k, d - 1], yr_r.at[k, d - 1], at_y(d))
 
     def zback_copy(k):
         n = source_of(k)
@@ -263,7 +291,7 @@
                 oexp[n] = value.astype(BF16)
                 zback_copy(k).start()
 
-        @pl.when(i >= 6)
+        @pl.when((i >= 6) & (i < NZ + 6))
         def _():
             k = i - 6
             n = (z + k) % NZ
@@ -272,24 +300,35 @@
             def _():
                 remote(oexp.at[n], back.at[n], b_s.at[k], b_r.at[k], at_z(k)).wait_recv()
 
-            acc[...] += dot_rows(comb_hi[n], back[n]) + dot_rows(comb_lo[n], back[n])
+            value = dot(spread[...], back[n]).astype(BF16)
+            ysend[n] = value.reshape(NY, TILE, width)
+
+            def send(d, inner):
+                yr(k, d).start()
+                return inner
+
+            lax.fori_loop(1, NY, send, 0)
+            yin[n, y] = ysend[n, y]
+
+        @pl.when(i >= 8)
+        def _():
+            k = i - 8
+            n = (z + k) % NZ
+
+            def arrive(d, inner):
+                block = yin.at[n, (y - d + NY) % NY]
+                remote(block, block, yr_s.at[k, d - 1], yr_r.at[k, d - 1], at_y(-d)).wait_recv()
+                return inner
+
+            lax.fori_loop(1, NY, arrive, 0)
+            value = yin[n].reshape(NY * TILE, width)
+            acc[...] += dot_rows(comb_hi[n], value) + dot_rows(comb_lo[n], value)
 
         return carry
 
-    acc[...] = jnp.zeros(acc.shape, F32)
-    lax.fori_loop(0, NZ + 6, stage, 0)
-
-    for q in range(NY):
-        ysend[q] = acc[q * nrow:(q + 1) * nrow, :].astype(BF16)
-    yr = []
-    for d in (4, 3, 5, 2, 6, 1, 7):
-        copy = remote(ysend.at[(y + d) % NY], yin.at[d - 1], yr_s.at[d - 1], yr_r.at[d - 1], at_y(d))
-        copy.start()
-        yr.append(copy)
-    total = proj[...] + acc[pl.ds(pl.multiple_of(y * nrow, nrow), nrow), :]
-    for d in range(1, NY):
-        remote(ysend.at[0], yin.at[d - 1], yr_s.at[d - 1], yr_r.at[d - 1], at_y(d)).wait_recv()
-        total = total + yin[d - 1].astype(F32)
+    lax.fori_loop(0, NZ + 8, stage, 0)
+
+    total = proj[...] + acc[pl.ds(pl.multiple_of(y % 2 * nrow, nrow), nrow), :]
 
     square = jnp.sum(total * total, axis=1, keepdims=True)
     ss_own[...] = jnp.broadcast_to(square, ss_own.shape)
@@ -304,7 +343,7 @@
     scale = lax.rsqrt(square / full + 1e-06)
     out[...] = (total * scale * gain[...]).astype(BF16)
 
-    for copy in meta_copies + rs_copies + yag + yr + ss:
+    for copy in meta_copies + rs_copies + yag + ss:
         copy.wait_send()
 
     def drain(k, carry):
@@ -317,7 +356,11 @@
             zsend_copy(k).wait_send()
             zback_copy(k).wait_send()
 
-        return carry
+        def sent(d, inner):
+            yr(k, d).wait_send()
+            return inner
+
+        return lax.fori_loop(1, NY, sent, carry)
 
     lax.fori_loop(0, NZ, drain, 0)
 
@@ -340,17 +383,18 @@
         pltpu.VMEM((nrow, width), F32),
         pltpu.VMEM((NY, 16, 2 * nrow), F32),
         pltpu.VMEM((NZ, chunk, NY * nrow), BF16),
-        pltpu.VMEM((NZ, chunk, NY * nrow), BF16),
-        pltpu.VMEM((NZ, chunk, NY * nrow), BF16),
+        pltpu.VMEM((NZ, NY * TILE, 2 * nrow), BF16),
+        pltpu.VMEM((NZ, NY * TILE, 2 * nrow), BF16),
+        pltpu.VMEM((NY * TILE, chunk), BF16),
         pltpu.VMEM((NY, nrow, width), BF16),
         pltpu.VMEM((NZ, chunk, width), BF16),
         pltpu.VMEM((NX, NZ, chunk, width), BF16),
         pltpu.VMEM((NX, NZ, chunk, hw), BF16),
         pltpu.VMEM((NZ, chunk, width), BF16),
         pltpu.VMEM((NZ, chunk, width), BF16),
-        pltpu.VMEM((NY * nrow, width), F32),
-        pltpu.VMEM((NY, nrow, width), BF16),
-        pltpu.VMEM((NY - 1, nrow, width), BF16),
+        pltpu.VMEM((2 * nrow, width), F32),
+        pltpu.VMEM((NZ, NY, TILE, width), BF16),
+        pltpu.VMEM((NZ, NY, TILE, width), BF16),
         pltpu.VMEM((nrow, 128), F32),
         pltpu.VMEM((NX - 1, nrow, 128), F32),
         dma((4,)),
@@ -363,7 +407,7 @@
         dma((NZ, 2)), dma((NZ, 2)),
         dma((NZ, 2)), dma((NZ, 2)),
         dma((NZ,)), dma((NZ,)),
-        dma((NY - 1,)), dma((NY - 1,)),
+        dma((NZ, NY - 1)), dma((NZ, NY - 1)),
         dma((NX - 1,)), dma((NX - 1,)),
     ]
     return pl.pallas_call(

time: 102 us -> 100 us (0.980)
  the two profiles are of different devices: /device:TPU:8 before, /device:TPU:16 now
where the time goes in v5:
time: 100 us
  Pallas kernels  98.7 us (99%)
  local copies, waits for them, and re-layouts  1.47 us (1%)
    pallas_call x1, Pallas kernels, body(): pl.pallas_call(kernel, out_shape=jax.ShapeDtypeStruct((nrow, width), BF16...  98.7 us

profile of v5, /device:TPU:16, one launch (start us, length us, event | category | flops | bytes accessed | tf_op | source)
XLA Modules:
  0.0 100.2 jit_solution(7828194609075085323)
XLA Ops:
  0.0 98.7 %shard_map.91 = bf16[64,512]{1,0:T(8,128)(2,1)} custom-call(bf16[64,512]{1,0:T(8,128)(2,1)} %attn.1, bf16[512,2048]{1,0:T(8,128)(2,1)} %w_out.1, bf16[64,512]{1,0:T(8,128)(2,1)} %resid.1, s32[6,64]{1,0:T(8,128)} %bitcast.9, f32[6,64]{1,0:T(8,128)} %bitcast.10, bf16[2048,256]{1,0:T(8,128)(2,1)} %bitcast.6, bf16[2048,256]{1,0:T(8,128)(2,1)} %bitcast.7, ...), custom_call_target="tpu_custom_call" | custom-call | tf_op jit(solution)/shard_map/pallas_call | solution.py:413
  98.7 1.5 %copy.11 = bf16[64,512]{1,0:T(8,128)(2,1)} copy(bf16[64,512]{1,0:T(8,128)(2,1)} %shard_map.91) | data formatting | bytes 131072
